TPU v7x, 32 devices: a whole 2x2x4 slice. The times are simulated.
32 devices in a mesh: pair: 4 (over x, core), blk: 8 (over z, y).
Axes of the slice: x: 2, y: 2, z: 4, core: 2. Of those that a mesh axis runs over, the one named last changes fastest.
Arguments:
- left_feats: bfloat16 [4, 64, 256, 256], P('pair', None, 'blk'), may hold values from -6 to 6
- right_feats: bfloat16 [4, 64, 256, 256], P('pair', None, 'blk'), may hold values from -6 to 6
- offsets: int32 [8], P('blk'), may hold values from 0 to 3, as said below
- hidden: bfloat16 [4, 64, 256, 128], P('pair', None, 'blk'), may hold values from -1 to 1
- context: bfloat16 [4, 3, 64, 256, 128], P('pair', None, None, 'blk'), may hold values from -6 to 6
- gru_weights: bfloat16 [2, 3, 5, 164, 128], replicated, may hold values from -0.21875 to 0.21875
- hidden_grad: float32 [4, 64, 256, 128], P('pair', None, 'blk'), may hold values from -0.06 to 0.06
Outputs:
- new_hidden: bfloat16 [4, 64, 256, 128], P('pair', None, 'blk')
- weight_grads: float32 [2, 3, 5, 164, 128], replicated
- hidden_in_grad: float32 [4, 64, 256, 128], P('pair', None, 'blk')
Inputs may be any that keep to these rules, and one draw needn't show every extreme that they name: Stripe s reads the frame-2 blocks s - offsets[s] - 1 and s - offsets[s]; some stripe has offset 4 - 1.
All inputs are finite; a program needn't handle non-finite values.
Results may differ from a plain program's by a relative error of at most 0.0054.
Values may be sent and summed in bfloat16 or wider, within the bound.
A program may use at most 128 MiB of HBM per device.

v0:
```python
import functools
import math
import jax
import jax.numpy as jnp
import numpy as np
from jax import lax
from jax.sharding import PartitionSpec as P

LEVELS = 4
RADIUS = 4


def with_halo(block, sides, width):
    for axis, dim in sides:
        count = lax.axis_size(axis)
        forward = [(i, i + 1) for i in range(count - 1)]
        backward = [(target, source) for source, target in forward]
        low = lax.ppermute(
            lax.slice_in_dim(block, block.shape[dim] - width, None, axis=dim), axis, forward
        )
        high = lax.ppermute(lax.slice_in_dim(block, 0, width, axis=dim), axis, backward)
        block = jnp.concatenate([low, block, high], axis=dim)
    return block


def lookup_table(column_count, level_count, radius_len):
    tap_count = 2 * radius_len + 1
    lookup = np.zeros((column_count, 2 * column_count, level_count * tap_count), np.float32)
    positions = np.arange(column_count)
    for level_id in range(level_count):
        pool_span = 2**level_id
        pooled_cols = 2 * column_count // pool_span
        for tap_id in range(tap_count):
            centre = (positions + column_count // 2) // pool_span + tap_id - radius_len
            inside = (centre >= 0) & (centre < pooled_cols)
            for inner_id in range(pool_span):
                lookup[
                    positions[inside],
                    centre[inside] * pool_span + inner_id,
                    level_id * tap_count + tap_id,
                ] = (1.0 / pool_span)
    return lookup


def tap_stack(padded, extent, axis_dim, kernel_len):
    return jnp.concatenate(
        [
            lax.slice_in_dim(padded, tap_id, tap_id + extent, axis=axis_dim)
            for tap_id in range(kernel_len)
        ],
        axis=-1,
    )


def conv_apply(padded, weight_taps, extent, axis_dim):
    kernel_len, in_chan, out_chan = weight_taps.shape
    stacked = tap_stack(padded, extent, axis_dim, kernel_len)
    flat_taps = stacked.reshape(-1, kernel_len * in_chan)
    result = jnp.dot(
        flat_taps,
        weight_taps.reshape(kernel_len * in_chan, out_chan),
        preferred_element_type=jnp.float32,
    )
    return result.reshape(stacked.shape[:-1] + (out_chan,))


def conv_weight_grad(padded, deltas, axis_dim):
    extent = deltas.shape[axis_dim]
    kernel_len = padded.shape[axis_dim] - extent + 1
    stacked = tap_stack(padded, extent, axis_dim, kernel_len)
    flat_taps = stacked.reshape(-1, stacked.shape[-1])
    flat_deltas = deltas.reshape(-1, deltas.shape[-1])
    result = lax.dot_general(
        flat_taps, flat_deltas, (((0,), (0,)), ((), ())), preferred_element_type=jnp.float32
    )
    return result.reshape(kernel_len, padded.shape[-1], deltas.shape[-1])


def conv_input_grad(deltas, weight_taps, axis_dim):
    kernel_len, in_chan, out_chan = weight_taps.shape
    backward_taps = lax.dot_general(
        deltas.reshape(-1, out_chan),
        weight_taps.reshape(kernel_len * in_chan, out_chan),
        (((1,), (1,)), ((), ())),
        preferred_element_type=jnp.float32,
    )
    backward_taps = backward_taps.reshape(deltas.shape[:-1] + (kernel_len * in_chan,))
    summed = None
    for tap_id in range(kernel_len):
        tap_part = backward_taps[..., tap_id * in_chan : (tap_id + 1) * in_chan]
        widths = [(0, 0)] * deltas.ndim
        widths[axis_dim] = (tap_id, kernel_len - 1 - tap_id)
        shifted = jnp.pad(tap_part, widths)
        summed = shifted if summed is None else summed + shifted
    return summed


def pad_along(values, axis_dim):
    widths = [(0, 0)] * values.ndim
    widths[axis_dim] = (2, 2)
    return jnp.pad(values, widths)


def crop_along(values, axis_dim):
    extent = values.shape[axis_dim] - 4
    return lax.slice_in_dim(values, 2, extent + 2, axis=axis_dim)


def section_forward(padded, context_parts, weights, axis_dim, extend):
    extent = padded.shape[axis_dim] - 4
    hidden_width = weights.shape[-1]
    own_inputs = lax.slice_in_dim(padded, 2, extent + 2, axis=axis_dim)
    hidden_own = own_inputs[..., :hidden_width].astype(jnp.float32)
    feat_padded = padded[..., hidden_width:]
    update_gate = jax.nn.sigmoid(
        conv_apply(padded, weights[0], extent, axis_dim) + context_parts[0].astype(jnp.float32)
    )
    reset_gate = jax.nn.sigmoid(
        conv_apply(padded, weights[1], extent, axis_dim) + context_parts[1].astype(jnp.float32)
    )
    reset_hidden = (reset_gate * hidden_own).astype(jnp.bfloat16)
    gated_padded = jnp.concatenate([extend(reset_hidden), feat_padded], axis=-1)
    candidate = jnp.tanh(
        conv_apply(gated_padded, weights[2], extent, axis_dim)
        + context_parts[2].astype(jnp.float32)
    )
    blended = (1.0 - update_gate) * hidden_own + update_gate * candidate
    return (blended, (update_gate, reset_gate, candidate, hidden_own, padded, gated_padded))


def section_backward(cotangent, stored, weights, axis_dim, fold_rims):
    update_gate, reset_gate, candidate, hidden_own, padded, gated_padded = stored
    hidden_width = weights.shape[-1]
    delta_cand = (cotangent * update_gate * (1.0 - candidate * candidate)).astype(jnp.bfloat16)
    grad_cand = conv_weight_grad(gated_padded, delta_cand, axis_dim)
    back_gated = fold_rims(conv_input_grad(delta_cand, weights[2][:, :hidden_width], axis_dim))
    delta_update = (
        cotangent * (candidate - hidden_own) * update_gate * (1.0 - update_gate)
    ).astype(jnp.bfloat16)
    delta_reset = (back_gated * hidden_own * reset_gate * (1.0 - reset_gate)).astype(jnp.bfloat16)
    grad_update = conv_weight_grad(padded, delta_update, axis_dim)
    grad_reset = conv_weight_grad(padded, delta_reset, axis_dim)
    grad_stack = jnp.stack([grad_update, grad_reset, grad_cand])
    back_inputs = conv_input_grad(
        delta_update, weights[0][:, :hidden_width], axis_dim
    ) + conv_input_grad(delta_reset, weights[1][:, :hidden_width], axis_dim)
    hidden_back = cotangent * (1.0 - update_gate) + back_gated * reset_gate + fold_rims(back_inputs)
    return (grad_stack, hidden_back)


def extend_gated(values):
    return with_halo(values, (("blk", 1),), 2)


def stripe_rims(values):
    extent = values.shape[1] - 4
    edge_terms = jnp.concatenate([values[:, :2], values[:, extent + 2 :]], axis=1)
    arrived = with_halo(edge_terms, (("blk", 1),), 2)
    own_terms = values[:, 2 : extent + 2]
    from_left = jnp.pad(arrived[:, :2], ((0, 0), (0, extent - 2), (0, 0)))
    from_right = jnp.pad(arrived[:, 6:], ((0, 0), (extent - 2, 0), (0, 0)))
    return own_terms + from_left + from_right


def on_device(left_feats, right_feats, offsets, hidden, context, gru_weights, hidden_grad):
    left_block = left_feats[0]
    right_block = right_feats[0]
    offset = offsets[0]
    stripe = lax.axis_index("blk")
    column_count = left_block.shape[1]
    empty_block = jnp.zeros_like(right_block)
    low_id = stripe - offset - 1
    high_id = stripe - offset
    shards = lax.all_gather(right_block, "blk", axis=1, tiled=True)
    shard_cols = shards.shape[1]

    def pick_one(slot_block, block_id):
        local_col = block_id * column_count
        usable = (local_col >= 0) & (local_col + column_count <= shard_cols)
        picked = lax.dynamic_slice_in_dim(
            shards, jnp.clip(local_col, 0, shard_cols - column_count), column_count, 1
        )
        return jnp.where(usable, picked, slot_block)

    low_block = pick_one(empty_block, low_id)
    high_block = pick_one(empty_block, high_id)
    window = jnp.concatenate([low_block, high_block], axis=1)
    scores = jnp.einsum("hxc,hjc->hxj", left_block, window, preferred_element_type=jnp.float32) * (
        1.0 / math.sqrt(left_block.shape[-1])
    )
    lookup = jnp.asarray(lookup_table(column_count, LEVELS, RADIUS))
    features = jnp.einsum("hxj,xjf->hxf", scores, lookup, precision=lax.Precision.HIGHEST).astype(
        jnp.bfloat16
    )
    context_parts = context[0]
    first_inputs = jnp.concatenate([hidden[0], features], axis=-1)
    first_padded = with_halo(first_inputs, (("blk", 1),), 2)
    first_new, first_stored = section_forward(
        first_padded, context_parts, gru_weights[0], 1, extend_gated
    )
    first_hidden = first_new.astype(jnp.bfloat16)
    second_inputs = jnp.concatenate([first_hidden, features], axis=-1)
    second_new, second_stored = section_forward(
        pad_along(second_inputs, 0),
        context_parts,
        gru_weights[1],
        0,
        functools.partial(pad_along, axis_dim=0),
    )
    second_grads, first_back = section_backward(
        hidden_grad[0], second_stored, gru_weights[1], 0, functools.partial(crop_along, axis_dim=0)
    )
    first_grads, hidden_back = section_backward(
        first_back, first_stored, gru_weights[0], 1, stripe_rims
    )
    grad_stack = lax.psum(jnp.stack([first_grads, second_grads]), ("pair", "blk"))
    return (second_new.astype(jnp.bfloat16)[None], grad_stack, hidden_back[None])


def solution(mesh):
    placed = (
        P("pair", None, "blk", None),
        P("pair", None, "blk", None),
        P("blk"),
        P("pair", None, "blk", None),
        P("pair", None, None, "blk", None),
        P(),
        P("pair", None, "blk", None),
    )
    return jax.shard_map(
        on_device,
        mesh=mesh,
        in_specs=placed,
        out_specs=(P("pair", None, "blk", None), P(), P("pair", None, "blk", None)),
        check_vma=False,
    )
```

profile of v0, /device:TPU:0, one launch (start us, length us, event | category | flops | bytes accessed | tf_op | source)
XLA Modules:
  0.0 494.4 jit_solution(1043420342084576107)
XLA Ops:
  8.6 129.2 %all-gather.3.cloned.1.call-done = bf16[1,64,256,256]{3,2,1,0:T(8,128)(2,1)} async-done(((bf16[1,64,32,256]{3,2,1,0:T(8,128)(2,1)}), bf16[1,64,256,256]{3,2,1,0:T(8,128)(2,1)}) %all-gather.3.cloned.1.call-update) | async-done | bytes 8388624 | tf_op jit(solution)/shard_map/all_gather | solution.py:174
  146.6 4.5 collective-permute-start
  158.5 7.6 %concatenate.75 = bf16[64,32,820]{2,1,0:T(8,128)(2,1)} concatenate(bf16[64,32,164]{2,1,0:T(8,128)(2,1)} %get-tuple-element.86, bf16[64,32,164]{2,1,0:T(8,128)(2,1)} %get-tuple-element.87, bf16[64,32,128]{2,1,0:T(8,128)(2,1)S(1)} %bitcast.177, bf16[64,32,36]{2,1,0:T(8,128)(2,1)S(1)} %copy.20, bf16[64,32,164]{2,1,0:T(8,128)(2,1)S(1)} %get-tuple-element.56, ...), dimensions={2} | concatenate | bytes 6717440 | tf_op jit(solution)/shard_map/concatenate | solution.py:46
  166.1 4.4 fusion.34
  172.5 5.6 %collective-permute-start.2 = (bf16[64,2,128]{2,1,0:T(2,128)(2,1)}, bf16[64,2,128]{2,1,0:T(2,128)(2,1)}, u32[]{:S(2)}, u32[]{:S(2)}) collective-permute-start(bf16[64,2,128]{2,1,0:T(2,128)(2,1)} %get-tuple-element.78), channel_id=1, source_target_pairs={{0,1},{1,2},{2,3},{3,4},{4,5},{5,6},{6,7},{8,9},{9,10},{10,11},{11... | collective-permute-start | bytes 98312 | tf_op jit(solution)/shard_map/ppermute | solution.py:18
  201.7 7.6 %concatenate.90 = bf16[2048,820]{1,0:T(8,128)(2,1)} concatenate(bf16[2048,164]{1,0:T(8,128)(2,1)} %bitcast.185, bf16[2048,164]{1,0:T(8,128)(2,1)} %bitcast.186, bf16[2048,128]{1,0:T(8,128)(2,1)S(1)} %bitcast.178, bf16[2048,36]{1,0:T(8,128)(2,1)S(1)} %bitcast.173, bf16[2048,164]{1,0:T(8,128)(2,1)S(1)} %bitcast.184, bf16[2048,164]{1,0:T(8,128)(2,1)S(1)} %bitcast.183), dimensions={1} | concatenate | bytes 6717440 | tf_op jit(solution)/shard_map/concatenate | solution.py:46
  209.3 6.0 %copy.32 = bf16[820,2048]{1,0:T(8,128)(2,1)} copy(bf16[820,2048]{0,1:T(8,128)(2,1)} %bitcast.182) | data formatting | bytes 6717440 | tf_op jit(solution)/shard_map/dot_general | solution.py:73
  215.4 4.3 reshape.193
  224.0 8.0 %concatenate.79 = bf16[64,32,820]{2,1,0:T(8,128)(2,1)} concatenate(bf16[64,32,164]{2,1,0:T(8,128)(2,1)} %get-tuple-element.54, bf16[64,32,164]{2,1,0:T(8,128)(2,1)} %get-tuple-element.53, bf16[64,32,164]{2,1,0:T(8,128)(2,1)} %get-tuple-element.52, bf16[64,32,164]{2,1,0:T(8,128)(2,1)S(1)} %get-tuple-element.51, bf16[64,32,164]{2,1,0:T(8,128)(2,1)S(1)} %get-tuple-element.50), dimensions={2} | concatenate | bytes 6717440 | tf_op jit(solution)/shard_map/concatenate | solution.py:46
  242.4 8.3 %concatenate.81 = bf16[64,32,820]{2,1,0:T(8,128)(2,1)} concatenate(bf16[64,32,164]{2,1,0:T(8,128)(2,1)} %get-tuple-element.73, bf16[64,32,164]{2,1,0:T(8,128)(2,1)} %get-tuple-element.71, bf16[64,32,128]{2,1,0:T(8,128)(2,1)} %copy-done.22, bf16[64,32,36]{2,1,0:T(8,128)(2,1)S(1)} %copy.20, bf16[64,32,164]{2,1,0:T(8,128)(2,1)} %get-tuple-element.72, ...), dimensions={2} | concatenate | bytes 6717440 | tf_op jit(solution)/shard_map/concatenate | solution.py:46
  250.6 4.5 fusion.16
  261.1 8.5 %concatenate.83 = bf16[64,32,820]{2,1,0:T(8,128)(2,1)} concatenate(bf16[64,32,164]{2,1,0:T(8,128)(2,1)} %get-tuple-element.69, bf16[64,32,164]{2,1,0:T(8,128)(2,1)} %get-tuple-element.68, bf16[64,32,164]{2,1,0:T(8,128)(2,1)} %get-tuple-element.67, bf16[64,32,164]{2,1,0:T(8,128)(2,1)} %get-tuple-element.66, bf16[64,32,164]{2,1,0:T(8,128)(2,1)} %get-tuple-element.65), dimensions={2} | concatenate | bytes 6717440 | tf_op jit(solution)/shard_map/concatenate | solution.py:46
  269.7 5.3 %fusion.48 = (bf16[64,32,128]{2,1,0:T(8,128)(2,1)S(1)}, bf16[64,32,128]{2,1,0:T(8,128)(2,1)S(1)}, bf16[1,64,32,128]{3,2,1,0:T(8,128)(2,1)}) fusion(f32[64,32,128]{2,1,0:T(8,128)} %fusion.16, bf16[64,32,128]{2,1,0:T(8,128)(2,1)S(1)} %copy-done.23, f32[1,64,32,128]{3,2,1,0:T(8,128)} %param.14, bf16[1,3,64,32,128]{4,3,2,1,0:T(8,128)(2,1)} %param.12, ...), kind=kOutput, calls=%fused_computation.80 | convolution fusion | flops 434634752 | bytes 8287232 | tf_op jit(solution)/shard_map/dot_general | solution.py:59
  290.7 6.0 %copy.35 = bf16[820,2048]{1,0:T(8,128)(2,1)} copy(bf16[820,2048]{0,1:T(8,128)(2,1)} %bitcast.181) | data formatting | bytes 6717440 | tf_op jit(solution)/shard_map/dot_general | solution.py:73
  296.7 4.2 reshape.208
  300.8 6.0 %copy.34 = bf16[820,2048]{1,0:T(8,128)(2,1)} copy(bf16[820,2048]{0,1:T(8,128)(2,1)} %bitcast.180) | data formatting | bytes 6717440 | tf_op jit(solution)/shard_map/dot_general | solution.py:73
  306.8 4.4 reshape.204
  311.3 4.0 convolution_bitcast_fusion.1
  317.1 6.0 %copy.33 = bf16[820,2048]{1,0:T(8,128)(2,1)} copy(bf16[820,2048]{0,1:T(8,128)(2,1)} %bitcast.174) | data formatting | bytes 6717440 | tf_op jit(solution)/shard_map/dot_general | solution.py:73
  323.1 4.2 reshape.201
  328.6 4.5 collective-permute-start.4
  350.9 5.7 %collective-permute-start.6 = (f32[64,2,128]{2,1,0:T(2,128)S(1)}, f32[64,2,128]{2,1,0:T(2,128)S(1)}, u32[]{:S(2)}, u32[]{:S(2)}) collective-permute-start(f32[64,2,128]{2,1,0:T(2,128)S(1)} %add_add_fusion.2), channel_id=1, source_target_pairs={{0,1},{1,2},{2,3},{3,4},{4,5},{5,6},{6,7},{8,9},{9,10},{10,11},{11... | collective-permute-start | bytes 196616 | tf_op jit(solution)/shard_map/ppermute | solution.py:18
  360.4 122.4 %all-reduce.38.cloned.1.call-done = f32[2,3,5,164,128]{4,3,2,1,0:T(8,128)} async-done(((f32[2,3,5,164,128]{4,3,2,1,0:T(8,128)}), f32[2,3,5,164,128]{4,3,2,1,0:T(8,128)}) %all-reduce.38.cloned.1.call-update) | async-done | bytes 2519056 | tf_op jit(solution)/shard_map/psum | solution.py:216
  482.8 4.5 copy.36
  (209 shorter events, 102.7 us)
Async XLA Ops:
  7.2 133.5 %copy-start = (bf16[1,64,32,256]{3,2,1,0:T(8,128)(2,1)S(1)}, bf16[1,64,32,256]{3,2,1,0:T(8,128)(2,1)}, u32[]{:S(2)}) copy-start(bf16[1,64,32,256]{3,2,1,0:T(8,128)(2,1)} %param.8) | copy-start | bytes 3145732
  7.2 130.7 %all-gather.3.cloned.1.call-start = ((), (), s32[]{:S(2)}) async-start(), calls=%async_computation.1 | async-start | bytes 9437184 | tf_op jit(solution)/shard_map/all_gather | solution.py:174
  7.9 474.8 %all-reduce.38.cloned.1.call-start = ((), (), s32[]{:S(2)}) async-start(), calls=%async_computation | async-start | bytes 5160960 | tf_op jit(solution)/shard_map/psum | solution.py:216
  141.7 9.4 %copy-start.17 = (bf16[2,3,5,164,128]{4,0,3,2,1:T(2,128)(2,1)S(1)}, bf16[2,3,5,164,128]{4,0,3,2,1:T(2,128)(2,1)}, u32[]{:S(2)}) copy-start(bf16[2,3,5,164,128]{4,0,3,2,1:T(2,128)(2,1)} %param.13) | copy-start | bytes 3778564
  145.3 9.6 %collective-permute-start.1 = (bf16[64,2,164]{2,1,0:T(2,128)(2,1)S(1)}, bf16[64,2,164]{2,1,0:T(2,128)(2,1)S(1)}, u32[]{:S(2)}, u32[]{:S(2)}) collective-permute-start(bf16[64,2,164]{2,1,0:T(2,128)(2,1)S(1)} %get-tuple-element.76), channel_id=1, source_target_pairs={{1,0},{2,1},{3,2},{4,3},{5,4},{6,5},{7,6},{9,8},{10,9},{11,10},{12... | collective-permute-start | bytes 125960 | tf_op jit(solution)/shard_map/ppermute | solution.py:21
  146.6 8.3 %collective-permute-start = (bf16[64,2,164]{2,1,0:T(2,128)(2,1)S(1)}, bf16[64,2,164]{2,1,0:T(2,128)(2,1)S(1)}, u32[]{:S(2)}, u32[]{:S(2)}) collective-permute-start(bf16[64,2,164]{2,1,0:T(2,128)(2,1)S(1)} %get-tuple-element.77), channel_id=1, source_target_pairs={{0,1},{1,2},{2,3},{3,4},{4,5},{5,6},{6,7},{8,9},{9,10},{10,11},{11... | collective-permute-start | bytes 125960 | tf_op jit(solution)/shard_map/ppermute | solution.py:18
  166.1 12.1 %copy-start.34 = (bf16[1,1,5,164,128]{4,0,3,2,1:T(2,128)(2,1)S(1)}, bf16[1,1,5,164,128]{4,0,3,2,1:T(2,128)(2,1)}, u32[]{:S(2)}) copy-start(bf16[1,1,5,164,128]{4,0,3,2,1:T(2,128)(2,1)} %get-tuple-element.59) | copy-start | bytes 629764
  166.1 12.8 %copy-start.33 = (bf16[1,1,5,164,128]{4,0,3,2,1:T(2,128)(2,1)S(1)}, bf16[1,1,5,164,128]{4,0,3,2,1:T(2,128)(2,1)}, u32[]{:S(2)}) copy-start(bf16[1,1,5,164,128]{4,0,3,2,1:T(2,128)(2,1)} %get-tuple-element.60) | copy-start | bytes 629764
  170.6 12.0 %copy-start.46 = (bf16[64,32,128]{2,1,0:T(8,128)(2,1)}, bf16[64,32,128]{2,1,0:T(8,128)(2,1)S(1)}, u32[]{:S(2)}) copy-start(bf16[64,32,128]{2,1,0:T(8,128)(2,1)S(1)} %get-tuple-element.80) | copy-start | bytes 1572868
  170.6 9.8 %copy-start.32 = (bf16[1,1,5,164,128]{4,0,3,2,1:T(2,128)(2,1)S(1)}, bf16[1,1,5,164,128]{4,0,3,2,1:T(2,128)(2,1)}, u32[]{:S(2)}) copy-start(bf16[1,1,5,164,128]{4,0,3,2,1:T(2,128)(2,1)} %get-tuple-element.61) | copy-start | bytes 629764
  170.6 11.2 %copy-start.31 = (bf16[1,1,5,164,128]{4,0,3,2,1:T(2,128)(2,1)S(1)}, bf16[1,1,5,164,128]{4,0,3,2,1:T(2,128)(2,1)}, u32[]{:S(2)}) copy-start(bf16[1,1,5,164,128]{4,0,3,2,1:T(2,128)(2,1)} %get-tuple-element.62) | copy-start | bytes 629764
  171.2 48.4 %collective-permute-start.3 = (bf16[64,2,128]{2,1,0:T(2,128)(2,1)}, bf16[64,2,128]{2,1,0:T(2,128)(2,1)S(1)}, u32[]{:S(2)}, u32[]{:S(2)}) collective-permute-start(bf16[64,2,128]{2,1,0:T(2,128)(2,1)} %get-tuple-element.79), channel_id=1, source_target_pairs={{1,0},{2,1},{3,2},{4,3},{5,4},{6,5},{7,6},{9,8},{10,9},{11,10},{12... | collective-permute-start | bytes 98312 | tf_op jit(solution)/shard_map/ppermute | solution.py:21
  172.5 47.1 %collective-permute-start.2 = (bf16[64,2,128]{2,1,0:T(2,128)(2,1)}, bf16[64,2,128]{2,1,0:T(2,128)(2,1)}, u32[]{:S(2)}, u32[]{:S(2)}) collective-permute-start(bf16[64,2,128]{2,1,0:T(2,128)(2,1)} %get-tuple-element.78), channel_id=1, source_target_pairs={{0,1},{1,2},{2,3},{3,4},{4,5},{5,6},{6,7},{8,9},{9,10},{10,11},{11... | collective-permute-start | bytes 98312 | tf_op jit(solution)/shard_map/ppermute | solution.py:18
  224.0 8.0 %copy-start.45 = (bf16[820,128,1]{1,0,2:T(8,128)(2,1)S(1)}, bf16[820,128,1]{1,0,2:T(8,128)(2,1)}, u32[]{:S(2)}) copy-start(bf16[820,128,1]{1,0,2:T(8,128)(2,1)} %reshape.226) | copy-start | bytes 629764
  237.9 47.4 %copy-start.11 = (f32[64,32,128]{2,1,0:T(8,128)}, f32[64,32,128]{2,1,0:T(8,128)S(1)}, u32[]{:S(2)}) copy-start(f32[64,32,128]{2,1,0:T(8,128)S(1)} %get-tuple-element.83) | copy-start | bytes 3145732
  323.1 10.1 %copy-start.48 = (bf16[5,128,128]{2,1,0:T(8,128)(2,1)S(1)}, bf16[5,128,128]{2,1,0:T(8,128)(2,1)}, u32[]{:S(2)}) copy-start(bf16[5,128,128]{2,1,0:T(8,128)(2,1)} %slice.423) | copy-start | bytes 491524
  327.3 14.4 %collective-permute-start.5 = (f32[64,2,128]{2,1,0:T(2,128)}, f32[64,2,128]{2,1,0:T(2,128)S(1)}, u32[]{:S(2)}, u32[]{:S(2)}) collective-permute-start(f32[64,2,128]{2,1,0:T(2,128)} %get-tuple-element.26), channel_id=1, source_target_pairs={{1,0},{2,1},{3,2},{4,3},{5,4},{6,5},{7,6},{9,8},{10,9},{11,10},{12... | collective-permute-start | bytes 196616 | tf_op jit(solution)/shard_map/ppermute | solution.py:21
  328.6 13.1 %collective-permute-start.4 = (f32[64,2,128]{2,1,0:T(2,128)S(1)}, f32[64,2,128]{2,1,0:T(2,128)S(1)}, u32[]{:S(2)}, u32[]{:S(2)}) collective-permute-start(f32[64,2,128]{2,1,0:T(2,128)S(1)} %get-tuple-element.25), channel_id=1, source_target_pairs={{0,1},{1,2},{2,3},{3,4},{4,5},{5,6},{6,7},{8,9},{9,10},{10,11},{11... | collective-permute-start | bytes 196616 | tf_op jit(solution)/shard_map/ppermute | solution.py:18
  349.4 9.0 %collective-permute-start.7 = (f32[64,2,128]{2,1,0:T(2,128)S(1)}, f32[64,2,128]{2,1,0:T(2,128)S(1)}, u32[]{:S(2)}, u32[]{:S(2)}) collective-permute-start(f32[64,2,128]{2,1,0:T(2,128)S(1)} %add_add_fusion.1), channel_id=1, source_target_pairs={{1,0},{2,1},{3,2},{4,3},{5,4},{6,5},{7,6},{9,8},{10,9},{11,10},{12... | collective-permute-start | bytes 196616 | tf_op jit(solution)/shard_map/ppermute | solution.py:21
  350.8 8.0 %copy-start.12 = (f32[64,32,128]{2,1,0:T(8,128)S(1)}, f32[64,32,128]{2,1,0:T(8,128)}, u32[]{:S(2)}) copy-start(f32[64,32,128]{2,1,0:T(8,128)} %copy-done.11) | copy-start | bytes 3145732
  350.9 8.0 %copy-start.14 = (f32[64,32,128]{2,1,0:T(8,128)S(1)}, f32[64,32,128]{2,1,0:T(8,128)}, u32[]{:S(2)}) copy-start(f32[64,32,128]{2,1,0:T(8,128)} %copy-done.13) | copy-start | bytes 3145732
  350.9 7.9 %copy-start.16 = (f32[64,36,128]{2,1,0:T(8,128)S(1)}, f32[64,36,128]{2,1,0:T(8,128)}, u32[]{:S(2)}) copy-start(f32[64,36,128]{2,1,0:T(8,128)} %pad_add_fusion) | copy-start | bytes 3538948
  350.9 7.9 %collective-permute-start.6 = (f32[64,2,128]{2,1,0:T(2,128)S(1)}, f32[64,2,128]{2,1,0:T(2,128)S(1)}, u32[]{:S(2)}, u32[]{:S(2)}) collective-permute-start(f32[64,2,128]{2,1,0:T(2,128)S(1)} %add_add_fusion.2), channel_id=1, source_target_pairs={{0,1},{1,2},{2,3},{3,4},{4,5},{5,6},{6,7},{8,9},{9,10},{10,11},{11... | collective-permute-start | bytes 196616 | tf_op jit(solution)/shard_map/ppermute | solution.py:18
  358.8 128.4 %copy-start.1 = (bf16[1,64,32,256]{3,2,1,0:T(8,128)(2,1)S(1)}, bf16[1,64,32,256]{3,2,1,0:T(8,128)(2,1)}, u32[]{:S(2)}) copy-start(bf16[1,64,32,256]{3,2,1,0:T(8,128)(2,1)} %param.8) | copy-start | bytes 3145732
  (46 other events, 124.1 us)
Sparse Core Ops, SparseCore 0:
  10.2 127.6 all-gather.2
  346.7 136.0 all-reduce.37
where the time goes:
time: 504 us; the launch traced here: 494 us
  waiting for transfers between devices  253 us (50%)
  local copies, waits for them, and re-layouts  141 us (28%)
  matrix products  41.8 us (8%)
  starting transfers between devices  25.7 us (5%)
  other arithmetic  17.8 us (4%)
  between operations  15.8 us (3%)
    all_gather x1, waiting for transfers between devices, on_device(): shards = lax.all_gather(right_block, 'blk', axis=1, tiled=True)  129 us
    psum x1, waiting for transfers between devices, on_device(): lax.psum(jnp.stack([first_grads, second_grads]), ('pair', 'blk'))  122 us
    concatenate x5, local copies, waits for them, and re-layouts, tap_stack(): jnp.concatenate([lax.slice_in_dim(padded, tap_id, tap_id + extent, axis=a...  40 us
    dot_general x4, local copies, waits for them, and re-layouts, conv_weight_grad(): lax.dot_general(flat_taps, flat_deltas, (((0,), (0,)), ((), ())), preferr...  24 us
    dot_general x6, matrix products, conv_apply(): jnp.dot(flat_taps, weight_taps.reshape(kernel_len * in_chan, out_chan), p...  23.4 us
    unnamed x133, local copies, waits for them, and re-layouts  22.1 us
    ppermute x4, starting transfers between devices, with_halo(): lax.ppermute(lax.slice_in_dim(block, block.shape[dim] - width, None, axis...  20.5 us
    another operation x4, local copies, waits for them, and re-layouts  17 us
  transfers between devices with their start and end apart: 10, of which 3 were waited for; matrix products, arithmetic and copies ran while one was open for 11% of the time, Pallas kernels for 0%

commit v1 on v0

--- a/solution.py
+++ b/solution.py
@@ -213,7 +213,9 @@
     first_grads, hidden_back = section_backward(
         first_back, first_stored, gru_weights[0], 1, stripe_rims
     )
-    grad_stack = lax.psum(jnp.stack([first_grads, second_grads]), ("pair", "blk"))
+    grad_stack = jnp.sum(
+        lax.all_gather(jnp.stack([first_grads, second_grads]), ("pair", "blk")), axis=0
+    )
     return (second_new.astype(jnp.bfloat16)[None], grad_stack, hidden_back[None])
 
 

time: 504 us -> 819 us (1.62)
  waiting for transfers between devices: 253 us -> 550 us
  other arithmetic: 17.8 us -> 44.1 us
    all_gather x0 -> x1, waiting for transfers between devices: none -> 414 us  [on_device(): lax.all_gather(jnp.stack([first_grads, second_grads]), ('pair', 'blk'))]
    psum x1 -> x0, waiting for transfers between devices: 122 us -> none  [on_device(): lax.psum(jnp.stack([first_grads, second_grads]), ('pair', 'blk'))]
    reduce_sum x0 -> x1, other arithmetic: none -> 26.9 us  [on_device(): jnp.sum(lax.all_gather(jnp.stack([first_grads, second_grads]), ('pair', '...]
    unnamed x133 -> x113, local copies, waits for them, and re-layouts: 22.1 us -> 20.7 us
  transfers between devices with their start and end apart: 10 -> 10, of which waited for: 3 -> 4; matrix products, arithmetic and copies ran while one was open for 11% -> 11% of each run, Pallas kernels for 0% -> 0%
where the time goes in v1:
time: 819 us; the launch traced here: 809 us
  waiting for transfers between devices  550 us (67%)
  local copies, waits for them, and re-layouts  134 us (16%)
  other arithmetic  44.1 us (5%)
  matrix products  44 us (5%)
  starting transfers between devices  21 us (3%)
  between operations  15.6 us (2%)
    all_gather x1, waiting for transfers between devices, on_device(): lax.all_gather(jnp.stack([first_grads, second_grads]), ('pair', 'blk'))  414 us
    all_gather x1, waiting for transfers between devices, on_device(): shards = lax.all_gather(right_block, 'blk', axis=1, tiled=True)  129 us
    concatenate x5, local copies, waits for them, and re-layouts, tap_stack(): jnp.concatenate([lax.slice_in_dim(padded, tap_id, tap_id + extent, axis=a...  39.9 us
    reduce_sum x1, other arithmetic, on_device(): jnp.sum(lax.all_gather(jnp.stack([first_grads, second_grads]), ('pair', '...  26.9 us
    dot_general x4, local copies, waits for them, and re-layouts, conv_weight_grad(): lax.dot_general(flat_taps, flat_deltas, (((0,), (0,)), ((), ())), preferr...  24.6 us
    dot_general x6, matrix products, conv_apply(): jnp.dot(flat_taps, weight_taps.reshape(kernel_len * in_chan, out_chan), p...  23.5 us
    unnamed x113, local copies, waits for them, and re-layouts  20.7 us
    another operation x4, local copies, waits for them, and re-layouts  16.7 us
  transfers between devices with their start and end apart: 10, of which 4 were waited for; matrix products, arithmetic and copies ran while one was open for 11% of the time, Pallas kernels for 0%

profile of v1, /device:TPU:0, one launch (start us, length us, event | category | flops | bytes accessed | tf_op | source)
XLA Modules:
  0.0 808.6 jit_solution(2934039970274298943)
XLA Ops:
  8.6 129.2 %all-gather.5.cloned.1.call-done = bf16[1,64,256,256]{3,2,1,0:T(8,128)(2,1)} async-done(((bf16[1,64,32,256]{3,2,1,0:T(8,128)(2,1)}), bf16[1,64,256,256]{3,2,1,0:T(8,128)(2,1)}) %all-gather.5.cloned.1.call-update) | async-done | bytes 8388624 | tf_op jit(solution)/shard_map/all_gather | solution.py:174
  157.7 7.6 concatenate.75
  165.3 4.4 fusion.40
  195.0 7.6 concatenate.90
  202.6 6.1 copy.48
  208.7 4.2 reshape.193
  217.3 7.9 concatenate.79
  234.4 8.2 %concatenate.81 = bf16[64,32,820]{2,1,0:T(8,128)(2,1)} concatenate(bf16[64,32,164]{2,1,0:T(8,128)(2,1)} %get-tuple-element.70, bf16[64,32,164]{2,1,0:T(8,128)(2,1)} %get-tuple-element.68, bf16[64,32,128]{2,1,0:T(8,128)(2,1)S(1)} %get-tuple-element.79, bf16[64,32,36]{2,1,0:T(8,128)(2,1)S(1)} %copy.36, bf16[64,32,164]{2,1,0:T(8,128)(2,1)} %get-tuple-element.69, ...), dimensions={2} | concatenate | bytes 6717440 | tf_op jit(solution)/shard_map/concatenate | solution.py:46
  242.6 4.4 fusion.50
  254.4 8.6 %concatenate.83 = bf16[64,32,820]{2,1,0:T(8,128)(2,1)} concatenate(bf16[64,32,164]{2,1,0:T(8,128)(2,1)} %get-tuple-element.66, bf16[64,32,164]{2,1,0:T(8,128)(2,1)} %get-tuple-element.65, bf16[64,32,164]{2,1,0:T(8,128)(2,1)} %get-tuple-element.64, bf16[64,32,164]{2,1,0:T(8,128)(2,1)} %get-tuple-element.63, bf16[64,32,164]{2,1,0:T(8,128)(2,1)} %get-tuple-element.62), dimensions={2} | concatenate | bytes 6717440 | tf_op jit(solution)/shard_map/concatenate | solution.py:46
  263.1 5.2 fusion.54
  282.6 4.5 collective-permute-start.4
  288.5 6.4 copy.49
  294.9 4.1 reshape.201
  299.1 6.0 copy.50
  305.1 4.2 reshape.204
  309.3 4.1 convolution_bitcast_fusion.2
  315.2 6.0 copy.51
  321.2 4.1 reshape.208
  341.6 4.7 collective-permute-start.6
  350.0 4.9 collective-permute-done.7
  356.5 413.8 %all-gather.7.cloned.1.call-done = f32[64,3,5,164,128]{4,3,2,1,0:T(8,128)} async-done(((f32[2,3,5,164,128]{4,3,2,1,0:T(8,128)}), f32[64,3,5,164,128]{4,3,2,1,0:T(8,128)}) %all-gather.7.cloned.1.call-update) | async-done | bytes 80609296 | tf_op jit(solution)/shard_map/all_gather | solution.py:217
  770.2 26.9 %reduce_sum.9 = f32[2,3,5,164,128]{4,3,2,1,0:T(8,128)} reduce(f32[32,2,3,5,164,128]{5,4,3,2,1,0:T(8,128)} %bitcast.59, f32[]{:T(128)} %constant.28.clone.1), dimensions={0}, to_apply=%region_0.1 | reduce | flops 19522560 | bytes 83128320 | tf_op jit(solution)/shard_map/reduce_sum | solution.py:216
  797.1 4.5 copy.52
  (190 shorter events, 105.2 us)
Async XLA Ops:
  7.2 133.6 %copy-start = (bf16[1,64,32,256]{3,2,1,0:T(8,128)(2,1)S(1)}, bf16[1,64,32,256]{3,2,1,0:T(8,128)(2,1)}, u32[]{:S(2)}) copy-start(bf16[1,64,32,256]{3,2,1,0:T(8,128)(2,1)} %param.8) | copy-start | bytes 3145732
  7.2 130.7 %all-gather.5.cloned.1.call-start = ((), (), s32[]{:S(2)}) async-start(), calls=%async_computation | async-start | bytes 9437184 | tf_op jit(solution)/shard_map/all_gather | solution.py:174
  7.9 762.3 %all-gather.7.cloned.1.call-start = ((), (), s32[]{:S(2)}) async-start(), calls=%async_computation.1 | async-start | bytes 85155840 | tf_op jit(solution)/shard_map/all_gather | solution.py:217
  141.9 7.3 copy-start.12
  145.4 7.4 collective-permute-start
  147.8 6.2 collective-permute-start.1
  165.2 9.9 %copy-start.27 = (bf16[1,1,5,164,128]{4,0,3,2,1:T(2,128)(2,1)S(1)}, bf16[1,1,5,164,128]{4,0,3,2,1:T(2,128)(2,1)}, u32[]{:S(2)}) copy-start(bf16[1,1,5,164,128]{4,0,3,2,1:T(2,128)(2,1)} %get-tuple-element.56) | copy-start | bytes 629764
  165.3 10.7 %copy-start.26 = (bf16[1,1,5,164,128]{4,0,3,2,1:T(2,128)(2,1)S(1)}, bf16[1,1,5,164,128]{4,0,3,2,1:T(2,128)(2,1)}, u32[]{:S(2)}) copy-start(bf16[1,1,5,164,128]{4,0,3,2,1:T(2,128)(2,1)} %get-tuple-element.57) | copy-start | bytes 629764
  169.7 9.9 %copy-start.37 = (bf16[64,32,128]{2,1,0:T(8,128)(2,1)}, bf16[64,32,128]{2,1,0:T(8,128)(2,1)S(1)}, u32[]{:S(2)}) copy-start(bf16[64,32,128]{2,1,0:T(8,128)(2,1)S(1)} %get-tuple-element.77) | copy-start | bytes 1572868
  169.7 7.7 copy-start.25
  169.7 9.2 %copy-start.24 = (bf16[1,1,5,164,128]{4,0,3,2,1:T(2,128)(2,1)S(1)}, bf16[1,1,5,164,128]{4,0,3,2,1:T(2,128)(2,1)}, u32[]{:S(2)}) copy-start(bf16[1,1,5,164,128]{4,0,3,2,1:T(2,128)(2,1)} %get-tuple-element.59) | copy-start | bytes 629764
  170.4 42.5 %collective-permute-start.2 = (bf16[64,2,128]{2,1,0:T(2,128)(2,1)}, bf16[64,2,128]{2,1,0:T(2,128)(2,1)S(1)}, u32[]{:S(2)}, u32[]{:S(2)}) collective-permute-start(bf16[64,2,128]{2,1,0:T(2,128)(2,1)} %get-tuple-element.75), channel_id=1, source_target_pairs={{0,1},{1,2},{2,3},{3,4},{4,5},{5,6},{6,7},{8,9},{9,10},{10,11},{11... | collective-permute-start | bytes 98312 | tf_op jit(solution)/shard_map/ppermute | solution.py:18
  173.7 39.2 %collective-permute-start.3 = (bf16[64,2,128]{2,1,0:T(2,128)(2,1)}, bf16[64,2,128]{2,1,0:T(2,128)(2,1)}, u32[]{:S(2)}, u32[]{:S(2)}) collective-permute-start(bf16[64,2,128]{2,1,0:T(2,128)(2,1)} %get-tuple-element.76), channel_id=1, source_target_pairs={{1,0},{2,1},{3,2},{4,3},{5,4},{6,5},{7,6},{9,8},{10,9},{11,10},{12... | collective-permute-start | bytes 98312 | tf_op jit(solution)/shard_map/ppermute | solution.py:21
  217.3 7.9 copy-start.36
  254.4 8.6 %copy-start.47 = (bf16[820,128,1]{1,0,2:T(8,128)(2,1)S(1)}, bf16[820,128,1]{1,0,2:T(8,128)(2,1)}, u32[]{:S(2)}) copy-start(bf16[820,128,1]{1,0,2:T(8,128)(2,1)} %reshape.230) | copy-start | bytes 629764
  263.1 5.2 copy-start.41
  268.3 4.6 copy-start.31
  282.6 49.2 %collective-permute-start.4 = (f32[64,2,128]{2,1,0:T(2,128)S(1)}, f32[64,2,128]{2,1,0:T(2,128)S(1)}, u32[]{:S(2)}, u32[]{:S(2)}) collective-permute-start(f32[64,2,128]{2,1,0:T(2,128)S(1)} %get-tuple-element.22), channel_id=1, source_target_pairs={{0,1},{1,2},{2,3},{3,4},{4,5},{5,6},{6,7},{8,9},{9,10},{10,11},{11... | collective-permute-start | bytes 196616 | tf_op jit(solution)/shard_map/ppermute | solution.py:18
  287.2 44.7 %collective-permute-start.5 = (f32[64,2,128]{2,1,0:T(2,128)S(1)}, f32[64,2,128]{2,1,0:T(2,128)S(1)}, u32[]{:S(2)}, u32[]{:S(2)}) collective-permute-start(f32[64,2,128]{2,1,0:T(2,128)S(1)} %get-tuple-element.23), channel_id=1, source_target_pairs={{1,0},{2,1},{3,2},{4,3},{5,4},{6,5},{7,6},{9,8},{10,9},{11,10},{12... | collective-permute-start | bytes 196616 | tf_op jit(solution)/shard_map/ppermute | solution.py:21
  341.6 8.3 %collective-permute-start.6 = (f32[64,2,128]{2,1,0:T(2,128)S(1)}, f32[64,2,128]{2,1,0:T(2,128)S(1)}, u32[]{:S(2)}, u32[]{:S(2)}) collective-permute-start(f32[64,2,128]{2,1,0:T(2,128)S(1)} %add_add_fusion.2), channel_id=1, source_target_pairs={{0,1},{1,2},{2,3},{3,4},{4,5},{5,6},{6,7},{8,9},{9,10},{10,11},{11... | collective-permute-start | bytes 196616 | tf_op jit(solution)/shard_map/ppermute | solution.py:18
  346.5 8.3 %copy-start.11 = (f32[64,36,128]{2,1,0:T(8,128)S(1)}, f32[64,36,128]{2,1,0:T(8,128)}, u32[]{:S(2)}) copy-start(f32[64,36,128]{2,1,0:T(8,128)} %pad_add_fusion) | copy-start | bytes 3538948
  346.6 8.3 %copy-start.20 = (f32[64,32,128]{2,1,0:T(8,128)S(1)}, f32[64,32,128]{2,1,0:T(8,128)}, u32[]{:S(2)}) copy-start(f32[64,32,128]{2,1,0:T(8,128)} %get-tuple-element.78) | copy-start | bytes 3145732
  346.6 8.3 %collective-permute-start.7 = (f32[64,2,128]{2,1,0:T(2,128)S(1)}, f32[64,2,128]{2,1,0:T(2,128)S(1)}, u32[]{:S(2)}, u32[]{:S(2)}) collective-permute-start(f32[64,2,128]{2,1,0:T(2,128)S(1)} %add_add_fusion.1), channel_id=1, source_target_pairs={{1,0},{2,1},{3,2},{4,3},{5,4},{6,5},{7,6},{9,8},{10,9},{11,10},{12... | collective-permute-start | bytes 196616 | tf_op jit(solution)/shard_map/ppermute | solution.py:21
  770.2 31.3 %copy-start.1 = (bf16[1,64,32,256]{3,2,1,0:T(8,128)(2,1)S(1)}, bf16[1,64,32,256]{3,2,1,0:T(8,128)(2,1)}, u32[]{:S(2)}) copy-start(bf16[1,64,32,256]{3,2,1,0:T(8,128)(2,1)} %param.8) | copy-start | bytes 3145732
  (36 other events, 81.4 us)
Sparse Core Ops, SparseCore 0:
  10.2 127.6 all-gather.4
  337.0 433.2 all-gather.6
